TPU v7x, 256 devices: a whole 4x4x8 slice. The times are simulated.
256 devices in a mesh: row: 16 (over z, core), col: 16 (over y, x).
Axes of the slice: x: 4, y: 4, z: 8, core: 2. Of those that a mesh axis runs over, the one named last changes fastest.
Arguments:
- clean_in: bfloat16 [512, 8192], P('row', 'col'), may hold values from -6 to 6
- corrupt_in: bfloat16 [512, 8192], P('row', 'col'), may hold values from -6 to 6
- patch_mask: int32 [512], replicated, may hold values 0 or 1
- gate_weight: bfloat16 [8192, 28672], P('col', 'row'), may hold values from -0.0625 to 0.0625
- up_weight: bfloat16 [8192, 28672], P('col', 'row'), may hold values from -0.0625 to 0.0625
- down_weight: bfloat16 [28672, 8192], P('row', 'col'), may hold values from -0.03125 to 0.03125
Outputs:
- clean_out: float32 [512, 8192], P('row', 'col')
- patched_out: float32 [512, 8192], P('row', 'col')
All inputs are finite; a program needn't handle non-finite values.
Results may differ from a plain program's by a relative error of at most 0.0029.
Values may be sent and summed in bfloat16 or wider, within the bound.
A program may use at most 128 MiB of HBM per device.

v0:
```python
import jax
import jax.numpy as jnp
from jax import lax
from jax.sharding import PartitionSpec as P


def on_device(clean_in, corrupt_in, patch_mask, gate_weight, up_weight, down_weight):
    stacked = jnp.stack((clean_in, corrupt_in), axis=1)
    piece = lax.all_gather(stacked, "row", axis=0, tiled=True)
    gate_part = jnp.einsum("tkd,df->tkf", piece, gate_weight, preferred_element_type=jnp.float32)
    up_part = jnp.einsum("tkd,df->tkf", piece, up_weight, preferred_element_type=jnp.float32)
    partial_sums = jnp.stack((gate_part, up_part), axis=2)
    summed = lax.psum_scatter(partial_sums, "col", scatter_dimension=0, tiled=True)
    row_count = summed.shape[0]
    row_mask = lax.dynamic_slice_in_dim(patch_mask, lax.axis_index("col") * row_count, row_count, 0)
    hidden = (jax.nn.silu(summed[:, :, 0]) * summed[:, :, 1]).astype(jnp.bfloat16)
    patched = jnp.where(row_mask[:, None] == 1, hidden[:, 0], hidden[:, 1])
    paired = jnp.stack((hidden[:, 0], patched), axis=1)
    gathered = lax.all_gather(paired, "col", axis=0, tiled=True)
    result = lax.psum_scatter(
        jnp.einsum("tkf,fd->tkd", gathered, down_weight, preferred_element_type=jnp.float32),
        "row",
        scatter_dimension=0,
        tiled=True,
    )
    return (result[:, 0], result[:, 1])


def solution(mesh):
    placed = (
        P("row", "col"),
        P("row", "col"),
        P(),
        P("col", "row"),
        P("col", "row"),
        P("row", "col"),
    )
    return jax.shard_map(
        on_device,
        mesh=mesh,
        in_specs=placed,
        out_specs=(P("row", "col"), P("row", "col")),
        check_vma=False,
    )
```

profile of v0, /device:TPU:1, one launch (start us, length us, event | category | flops | bytes accessed | tf_op | source)
XLA Modules:
  0.0 308.9 jit_solution(6040133685950640488)
XLA Ops:
  7.2 0.0 copy-start
  7.2 0.0 all-gather.3.cloned.1.call-start
  7.2 1.5 pad_maximum_fusion.2
  8.8 0.0 all-gather.3.cloned.1.call-update
  8.8 0.0 reduce-scatter.3.cloned.1.call-start
  8.8 44.4 %all-gather.3.cloned.1.call-done = bf16[512,2,512]{2,0,1:T(8,128)(2,1)} async-done(((bf16[32,2,512]{2,0,1:T(8,128)(2,1)}), bf16[512,2,512]{2,0,1:T(8,128)(2,1)}) %all-gather.3.cloned.1.call-update) | async-done | bytes 1048592 | tf_op jit(solution)/shard_map/all_gather | solution.py:9
  53.2 0.0 copy-done
  53.2 0.0 copy-start.1
  53.2 0.0 copy-start.2
  53.2 6.4 %convolution_bitcast_fusion = f32[512,2,1,1792]{3,0,1,2:T(8,128)} fusion(bf16[512,2,512]{2,0,1:T(8,128)(2,1)} %all-gather.3.cloned.1.call-done, bf16[512,1792]{1,0:T(8,128)(2,1)S(1)} %copy-done), kind=kOutput, calls=%fused_computation.1 | convolution fusion | flops 1879048192 | bytes 10223616 | tf_op jit(solution)/shard_map/tkd,df->tkf/dot_general | solution.py:11
  59.6 0.0 copy-done.1
  59.6 0.0 copy-done.2
  59.6 5.0 %convolution_bitcast_fusion.1 = f32[512,2,1,1792]{3,0,1,2:T(8,128)} fusion(bf16[512,2,512]{2,0,1:T(8,128)(2,1)S(1)} %copy-done.2, bf16[512,1792]{1,0:T(8,128)(2,1)S(1)} %copy-done.1), kind=kOutput, calls=%fused_computation.2 | convolution fusion | flops 1879048192 | bytes 10223616 | tf_op jit(solution)/shard_map/tkd,df->tkf/dot_general | solution.py:10
  64.6 11.9 %pad_maximum_fusion = f32[512,2,2,1792]{3,0,1,2:T(8,128)} fusion(f32[512,2,1,1792]{3,0,1,2:T(8,128)} %convolution_bitcast_fusion, f32[512,2,1,1792]{3,0,1,2:T(8,128)} %convolution_bitcast_fusion.1), kind=kLoop, calls=%fused_computation | loop fusion | flops 3670016 | bytes 29360128 | tf_op jit(solution)/shard_map/stack | solution.py:12
  76.5 0.0 reduce-scatter.3.cloned.1.call-update
  76.5 0.0 all-gather.5.cloned.1.call-start
  76.6 0.8 dynamic-slice_compare_fusion
  77.3 105.0 %reduce-scatter.3.cloned.1.call-done = f32[32,2,2,1792]{3,0,1,2:T(8,128)} async-done(((f32[512,2,2,1792]{3,0,1,2:T(8,128)}), f32[32,2,2,1792]{3,0,1,2:T(8,128)}) %reduce-scatter.3.cloned.1.call-update) | async-done | bytes 917520 | tf_op jit(solution)/shard_map/reduce_scatter | solution.py:13
  182.3 1.3 fusion.5
  183.6 0.1 fusion.6
  183.7 0.7 pad_maximum_fusion.1
  184.4 0.0 all-gather.5.cloned.1.call-update
  184.4 0.0 reduce-scatter.5.cloned.1.call-start
  184.5 53.5 %all-gather.5.cloned.1.call-done = bf16[512,2,1792]{2,0,1:T(8,128)(2,1)} async-done(((bf16[32,2,1792]{2,0,1:T(8,128)(2,1)}), bf16[512,2,1792]{2,0,1:T(8,128)(2,1)}) %all-gather.5.cloned.1.call-update) | async-done | bytes 3670032 | tf_op jit(solution)/shard_map/all_gather | solution.py:19
  238.0 6.0 %fusion = f32[512,2,512]{2,0,1:T(8,128)} fusion(bf16[512,2,1792]{2,0,1:T(8,128)(2,1)} %all-gather.5.cloned.1.call-done, bf16[1792,512]{1,0:T(8,128)(2,1)} %param.11), kind=kOutput, calls=%fused_computation.3 | convolution fusion | flops 1879048192 | bytes 7602176 | tf_op jit(solution)/shard_map/tkf,fd->tkd/dot_general | solution.py:21
  244.0 0.0 reduce-scatter.5.cloned.1.call-update
  244.0 56.9 %reduce-scatter.5.cloned.1.call-done = f32[32,2,512]{2,0,1:T(8,128)} async-done(((f32[512,2,512]{2,0,1:T(8,128)}), f32[32,2,512]{2,0,1:T(8,128)}) %reduce-scatter.5.cloned.1.call-update) | async-done | bytes 131088 | tf_op jit(solution)/shard_map/reduce_scatter | solution.py:20
  300.9 1.5 slice_bitcast_fusion.2
Async XLA Ops:
  7.2 46.0 %copy-start = (bf16[512,1792]{1,0:T(8,128)(2,1)S(1)}, bf16[512,1792]{1,0:T(8,128)(2,1)}, u32[]{:S(2)}) copy-start(bf16[512,1792]{1,0:T(8,128)(2,1)} %param.10) | copy-start | bytes 5505028
  7.2 46.0 %all-gather.3.cloned.1.call-start = ((), (), s32[]{:S(2)}) async-start(), calls=%async_computation.2 | async-start | bytes 1114112 | tf_op jit(solution)/shard_map/all_gather | solution.py:9
  8.8 173.5 %reduce-scatter.3.cloned.1.call-start = ((), (), s32[]{:S(2)}) async-start(), calls=%async_computation.3 | async-start | bytes 15597568 | tf_op jit(solution)/shard_map/reduce_scatter | solution.py:13
  53.2 6.4 %copy-start.1 = (bf16[512,1792]{1,0:T(8,128)(2,1)S(1)}, bf16[512,1792]{1,0:T(8,128)(2,1)}, u32[]{:S(2)}) copy-start(bf16[512,1792]{1,0:T(8,128)(2,1)} %param.9) | copy-start | bytes 5505028
  53.2 6.4 %copy-start.2 = (bf16[512,2,512]{2,0,1:T(8,128)(2,1)S(1)}, bf16[512,2,512]{2,0,1:T(8,128)(2,1)}, u32[]{:S(2)}) copy-start(bf16[512,2,512]{2,0,1:T(8,128)(2,1)} %all-gather.3.cloned.1.call-done) | copy-start | bytes 3145732
  76.5 161.5 %all-gather.5.cloned.1.call-start = ((), (), s32[]{:S(2)}) async-start(), calls=%async_computation.4 | async-start | bytes 3899392 | tf_op jit(solution)/shard_map/all_gather | solution.py:19
  184.4 116.5 %reduce-scatter.5.cloned.1.call-start = ((), (), s32[]{:S(2)}) async-start(), calls=%async_computation.5 | async-start | bytes 2228224 | tf_op jit(solution)/shard_map/reduce_scatter | solution.py:20
Sparse Core Ops, SparseCore 0:
  10.4 42.7 all-gather.2
  76.6 105.6 reduce-scatter.2
  184.7 53.2 all-gather.4
  244.1 56.7 reduce-scatter.4
where the time goes:
time: 311 us; the launch traced here: 309 us
  waiting for transfers between devices  260 us (84%)
  matrix products  17.4 us (6%)
  other arithmetic  16.3 us (5%)
  between operations  13.8 us (4%)
    reduce_scatter x1, waiting for transfers between devices, on_device(): lax.psum_scatter(partial_sums, 'col', scatter_dimension=0, tiled=True)  105 us
    reduce_scatter x1, waiting for transfers between devices, on_device(): lax.psum_scatter(jnp.einsum('tkf,fd->tkd', gathered, down_weight, preferr...  56.9 us
    all_gather x1, waiting for transfers between devices, on_device(): gathered = lax.all_gather(paired, 'col', axis=0, tiled=True)  53.5 us
    all_gather x1, waiting for transfers between devices, on_device(): piece = lax.all_gather(stacked, 'row', axis=0, tiled=True)  44.4 us
    another operation x1, other arithmetic, on_device(): partial_sums = jnp.stack((gate_part, up_part), axis=2)  11.9 us
    dot_general x1, matrix products, on_device(): jnp.einsum('tkd,df->tkf', piece, up_weight, preferred_element_type=jnp.fl...  6.36 us
  transfers between devices with their start and end apart: 4, of which 4 were waited for; matrix products, arithmetic and copies ran while one was open for 0% of the time, Pallas kernels for 0%

commit v1 on v0

v1 whole, which is shorter than its diff:
```python
import jax
import jax.numpy as jnp
from jax import lax
from jax.experimental import pallas as pl
from jax.experimental.pallas import tpu as pltpu
from jax.sharding import PartitionSpec as P

MESH = pl.DeviceIdType.MESH
ZN = 8
XN = 4


def remote(src, dst, send, recv, axis, index):
    return pltpu.make_async_remote_copy(
        src_ref=src, dst_ref=dst, send_sem=send, recv_sem=recv,
        device_id={axis: index}, device_id_type=MESH,
    )


def greet(axis, peers):
    barrier = pltpu.get_barrier_semaphore()
    for peer in peers:
        pl.semaphore_signal(barrier, inc=1, device_id={axis: peer}, device_id_type=MESH)
    pl.semaphore_wait(barrier, len(peers))


def gather_row_kernel(clean_ref, corrupt_ref, out_ref, local_sem, send_sem, recv_sem, pair_send, pair_recv):
    me = lax.axis_index("row")
    z, core = me // 2, me % 2
    right = ((z + 1) % ZN) * 2 + core
    left = ((z + ZN - 1) % ZN) * 2 + core
    pair = z * 2 + (1 - core)
    first = pltpu.make_async_copy(clean_ref, out_ref.at[me, 0], local_sem.at[0])
    second = pltpu.make_async_copy(corrupt_ref, out_ref.at[me, 1], local_sem.at[1])
    first.start()
    second.start()
    greet("row", (left, right, pair))
    first.wait()
    second.wait()

    def chain(way, step, block):
        view = out_ref.at[block] if step < 3 else out_ref.at[block, way]
        return remote(view, view, send_sem.at[way, step], recv_sem.at[way, step], "row", (right, left)[way])

    def hand(slot, view):
        return remote(view, view, pair_send.at[slot], pair_recv.at[slot], "row", pair)

    started = []

    def go(copy):
        copy.start()
        started.append(copy)

    go(chain(0, 0, me))
    go(chain(1, 0, me))
    go(hand(0, out_ref.at[me]))
    for step in range(4):
        for way in range(2):
            away = (ZN - step - 1) if way == 0 else (step + 1)
            block = ((z + away) % ZN) * 2 + core
            chain(way, step, block).wait_recv()
            if step < 3:
                go(chain(way, step + 1, block))
            view = out_ref.at[block] if step < 3 else out_ref.at[block, way]
            go(hand(1 + step * 2 + way, view))
    hand(0, out_ref.at[pair]).wait_recv()
    for step in range(4):
        for way in range(2):
            away = (ZN - step - 1) if way == 0 else (step + 1)
            block = ((z + away) % ZN) * 2 + (1 - core)
            view = out_ref.at[block] if step < 3 else out_ref.at[block, way]
            hand(1 + step * 2 + way, view).wait_recv()
    for copy in started:
        copy.wait_send()


def gather_row(clean, corrupt):
    rows, width = clean.shape
    return pl.pallas_call(
        gather_row_kernel,
        out_shape=jax.ShapeDtypeStruct((2 * ZN, 2, rows, width), clean.dtype),
        in_specs=[pl.BlockSpec(memory_space=pl.ANY)] * 2,
        out_specs=pl.BlockSpec(memory_space=pltpu.VMEM),
        scratch_shapes=[
            pltpu.SemaphoreType.DMA((2,)),
            pltpu.SemaphoreType.DMA((2, 4)),
            pltpu.SemaphoreType.DMA((2, 4)),
            pltpu.SemaphoreType.DMA((9,)),
            pltpu.SemaphoreType.DMA((9,)),
        ],
        compiler_params=pltpu.CompilerParams(collective_id=0, has_side_effects=True),
        name="gather_row",
    )(clean, corrupt)


def gather_col_kernel(own_ref, out_ref, local_sem, send_sem, recv_sem):
    me = lax.axis_index("col")
    y, x = me // XN, me % XN
    half = own_ref.shape[1] // 2

    def at(dy, dx):
        return ((y + dy) % XN) * XN + (x + dx) % XN

    local = pltpu.make_async_copy(own_ref, out_ref.at[me], local_sem.at[0])
    local.start()
    greet("col", (at(0, 1), at(0, XN - 1), at(1, 0), at(XN - 1, 0)))
    local.wait()

    started = []

    def neighbour(run, stage, way):
        step = 1 if way == 0 else XN - 1
        along_x = (run + stage) % 2 == 0
        return at(0, step) if along_x else at(step, 0)

    def block_of(run, lane, hop):
        return at(hop, lane) if run == 0 else at(lane, hop)

    def copy_of(run, group, way, far, block):
        stage = 0 if group == 0 else 1
        view = out_ref.at[block, run]
        if far:
            view = out_ref.at[block, run, pl.ds(way * half, half)]
        sems = (run, group, way * 2 + far)
        return remote(view, view, send_sem.at[sems], recv_sem.at[sems], "col", neighbour(run, stage, way))

    def go(*key):
        copy = copy_of(*key)
        copy.start()
        started.append(copy)

    def second(run, lane):
        block = block_of(run, lane, 0)
        for way in range(2):
            go(run, 1 + lane, way, 0, block)

    for run in range(2):
        for way in range(2):
            go(run, 0, way, 0, me)
    for run in range(2):
        second(run, 0)
    for way in range(2):
        lane = XN - 1 if way == 0 else 1
        for run in range(2):
            block = block_of(run, lane, 0)
            copy_of(run, 0, way, 0, block).wait_recv()
            go(run, 0, way, 1, block)
            second(run, lane)

    def relay(run, lane):
        for way in range(2):
            hop = XN - 1 if way == 0 else 1
            block = block_of(run, lane, hop)
            copy_of(run, 1 + lane, way, 0, block).wait_recv()
            go(run, 1 + lane, way, 1, block)

    for run in range(2):
        relay(run, 0)
    for run in range(2):
        block = block_of(run, 2, 0)
        for way in range(2):
            copy_of(run, 0, way, 1, block).wait_recv()
        second(run, 2)
    for lane in (3, 1, 2):
        for run in range(2):
            relay(run, lane)
    for lane in range(XN):
        for run in range(2):
            for way in range(2):
                copy_of(run, 1 + lane, way, 1, block_of(run, lane, 2)).wait_recv()
    for copy in started:
        copy.wait_send()


def gather_col(paired):
    return pl.pallas_call(
        gather_col_kernel,
        out_shape=jax.ShapeDtypeStruct((XN * XN,) + paired.shape, paired.dtype),
        in_specs=[pl.BlockSpec(memory_space=pl.ANY)],
        out_specs=pl.BlockSpec(memory_space=pltpu.VMEM),
        scratch_shapes=[
            pltpu.SemaphoreType.DMA((1,)),
            pltpu.SemaphoreType.DMA((2, 1 + XN, 4)),
            pltpu.SemaphoreType.DMA((2, 1 + XN, 4)),
        ],
        compiler_params=pltpu.CompilerParams(collective_id=1, has_side_effects=True),
        name="gather_col",
    )(paired)


def scatter_row_kernel(part_ref, clean_ref, patched_ref, pair_buf, out_buf, in_buf, pair_send, pair_recv, send_sem, recv_sem):
    me = lax.axis_index("row")
    z, core = me // 2, me % 2
    pair = z * 2 + (1 - core)
    peers = [((z + d) % ZN) * 2 + core for d in range(1, ZN)]
    greet("row", [pair] + peers)
    order = (4, 3, 5, 2, 6, 1, 7, 0)

    def hand(d):
        target = ((z + d) % ZN) * 2 + (1 - core)
        return remote(part_ref.at[target], pair_buf.at[d], pair_send.at[d], pair_recv.at[d], "row", pair)

    def cast(d):
        return remote(out_buf.at[d], in_buf.at[d], send_sem.at[d], recv_sem.at[d], "row", ((z + d) % ZN) * 2 + core)

    for d in order:
        hand(d).start()
    for d in order[:-1]:
        hand(d).wait_recv()
        mine = ((z + d) % ZN) * 2 + core
        out_buf[d] = (part_ref[mine] + pair_buf[d]).astype(out_buf.dtype)
        cast(d).start()
    hand(0).wait_recv()
    total = part_ref[me] + pair_buf[0]
    clean_ref[...] = total[0]
    patched_ref[...] = total[1]
    for d in (1, 7, 2, 6, 3, 5, 4):
        cast(d).wait_recv()
        clean_ref[...] += in_buf[d, 0].astype(jnp.float32)
        patched_ref[...] += in_buf[d, 1].astype(jnp.float32)
    for d in range(ZN):
        hand(d).wait_send()
    for d in range(1, ZN):
        cast(d).wait_send()


def scatter_row(part):
    block = part.shape[1:]
    out = jax.ShapeDtypeStruct(block[1:], jnp.float32)
    return pl.pallas_call(
        scatter_row_kernel,
        out_shape=(out, out),
        in_specs=[pl.BlockSpec(memory_space=pltpu.VMEM)],
        out_specs=(pl.BlockSpec(memory_space=pltpu.VMEM), pl.BlockSpec(memory_space=pltpu.VMEM)),
        scratch_shapes=[
            pltpu.VMEM((ZN,) + block, jnp.float32),
            pltpu.VMEM((ZN,) + block, jnp.bfloat16),
            pltpu.VMEM((ZN,) + block, jnp.bfloat16),
            pltpu.SemaphoreType.DMA((ZN,)),
            pltpu.SemaphoreType.DMA((ZN,)),
            pltpu.SemaphoreType.DMA((ZN,)),
            pltpu.SemaphoreType.DMA((ZN,)),
        ],
        compiler_params=pltpu.CompilerParams(collective_id=2, has_side_effects=True),
        name="scatter_row",
    )(part)


def on_device(clean_in, corrupt_in, patch_mask, gate_weight, up_weight, down_weight):
    rows, width = clean_in.shape
    piece = gather_row(clean_in, corrupt_in).reshape(-1, width)
    gate_part = jnp.dot(piece, gate_weight, preferred_element_type=jnp.float32)
    gate = lax.psum_scatter(gate_part, "col", scatter_dimension=0, tiled=True)
    up_part = jnp.dot(piece, up_weight, preferred_element_type=jnp.float32)
    up = lax.psum_scatter(up_part, "col", scatter_dimension=0, tiled=True)
    row_mask = lax.dynamic_slice_in_dim(patch_mask, lax.axis_index("col") * rows, rows, 0)
    hidden = (jax.nn.silu(gate) * up).astype(jnp.bfloat16).reshape(2, rows, -1)
    patched = jnp.where(row_mask[:, None] == 1, hidden[0], hidden[1])
    gathered = gather_col(jnp.stack((hidden[0], patched)))
    part = jnp.dot(gathered.reshape(-1, gathered.shape[-1]), down_weight, preferred_element_type=jnp.float32)
    return scatter_row(part.reshape(2 * ZN, 2, rows, -1))


def solution(mesh):
    placed = (
        P("row", "col"),
        P("row", "col"),
        P(),
        P("col", "row"),
        P("col", "row"),
        P("row", "col"),
    )
    return jax.shard_map(
        on_device,
        mesh=mesh,
        in_specs=placed,
        out_specs=(P("row", "col"), P("row", "col")),
        check_vma=False,
    )
```

time: 311 us -> 282 us (0.907)
  waiting for transfers between devices: 260 us -> 170 us
  Pallas kernels: 0 us -> 71.9 us
  other arithmetic: 16.3 us -> 2.85 us
    all_gather x2 -> x0, waiting for transfers between devices: 97.9 us -> none  [the longest x1 53.5 us: on_device(): gathered = lax.all_gather(paired, 'col', axis=0, tiled=True)]
    pallas_call x0 -> x3, Pallas kernels: none -> 71.9 us  [the longest x1 25.7 us: scatter_row(): pl.pallas_call(scatter_row_kernel, out_shape=(out, out), in_specs=[pl.Blo...]
    another operation x3 -> x1, other arithmetic: 14.1 us -> 0.72 us  [on_device(): gathered = gather_col(jnp.stack((hidden[0], patched)))]
    reduce_scatter x2, waiting for transfers between devices: 162 us -> 170 us  [the longest x1 91.9 us: on_device(): gate = lax.psum_scatter(gate_part, 'col', scatter_dimension=0, tiled=True)]
    unnamed x6, local copies, waits for them, and re-layouts: 0.02 us -> 4.11 us
  transfers between devices with their start and end apart: 4 -> 2, of which waited for: 4 -> 2; matrix products, arithmetic and copies ran while one was open for 0% -> 3% of each run, Pallas kernels for 0% -> 0%
where the time goes in v1:
time: 282 us
  waiting for transfers between devices  170 us (60%)
  Pallas kernels  71.9 us (25%)
  matrix products  18.8 us (7%)
  between operations  14.1 us (5%)
  local copies, waits for them, and re-layouts  4.11 us (1%)
  other arithmetic  2.85 us (1%)
    reduce_scatter x1, waiting for transfers between devices, on_device(): gate = lax.psum_scatter(gate_part, 'col', scatter_dimension=0, tiled=True)  91.9 us
    reduce_scatter x1, waiting for transfers between devices, on_device(): up = lax.psum_scatter(up_part, 'col', scatter_dimension=0, tiled=True)  77.9 us
    pallas_call x1, Pallas kernels, scatter_row(): pl.pallas_call(scatter_row_kernel, out_shape=(out, out), in_specs=[pl.Blo...  25.7 us
    pallas_call x1, Pallas kernels, gather_col(): pl.pallas_call(gather_col_kernel, out_shape=jax.ShapeDtypeStruct((XN * XN...  23.6 us
    pallas_call x1, Pallas kernels, gather_row(): pl.pallas_call(gather_row_kernel, out_shape=jax.ShapeDtypeStruct((2 * ZN,...  22.6 us
    dot_general x1, matrix products, on_device(): gate_part = jnp.dot(piece, gate_weight, preferred_element_type=jnp.float32)  6.59 us
    dot_general x1, matrix products, on_device(): up_part = jnp.dot(piece, up_weight, preferred_element_type=jnp.float32)  6.24 us
    dot_general x1, matrix products, on_device(): jnp.dot(gathered.reshape(-1, gathered.shape[-1]), down_weight, preferred_...  6.01 us
  transfers between devices with their start and end apart: 2, of which 2 were waited for; matrix products, arithmetic and copies ran while one was open for 3% of the time, Pallas kernels for 0%

profile of v1, /device:TPU:1, one launch (start us, length us, event | category | flops | bytes accessed | tf_op | source)
XLA Modules:
  0.0 281.7 jit_solution(7250554421411012514)
XLA Ops:
  7.2 0.0 copy-start
  7.2 0.0 reduce-scatter.5.cloned.1.call-start
  7.2 22.6 %gather_row.1 = bf16[16,2,32,512]{3,2,1,0:T(8,128)(2,1)} custom-call(bf16[32,512]{1,0:T(8,128)(2,1)} %clean_ref.1, bf16[32,512]{1,0:T(8,128)(2,1)} %corrupt_ref.1), custom_call_target="tpu_custom_call" | custom-call | tf_op jit(solution)/shard_map/gather_row/pallas_call | solution.py:79
  29.8 0.0 copy-done
  29.9 6.2 %fusion.4 = f32[1024,1792]{1,0:T(8,128)} fusion(bf16[1024,512]{1,0:T(8,128)(2,1)} %bitcast.15, bf16[512,1792]{1,0:T(8,128)(2,1)S(1)} %copy-done), kind=kOutput, calls=%fused_computation.9 | convolution fusion | flops 1879048192 | bytes 10223616 | tf_op jit(solution)/shard_map/dot_general | solution.py:254
  36.1 0.0 copy-start.1
  36.1 0.0 reduce-scatter.5.cloned.1.call-update
  36.1 0.0 reduce-scatter.3.cloned.1.call-start
  36.2 1.1 copy-done.1
  37.3 6.6 %fusion.3 = f32[1024,1792]{1,0:T(8,128)} fusion(bf16[1024,512]{1,0:T(8,128)(2,1)S(1)} %bitcast.16, bf16[512,1792]{1,0:T(8,128)(2,1)} %param.9), kind=kOutput, calls=%fused_computation.8 | convolution fusion | flops 1879048192 | bytes 10223616 | tf_op jit(solution)/shard_map/dot_general | solution.py:252
  43.9 0.0 reduce-scatter.3.cloned.1.call-update
  43.9 0.8 dynamic-slice_compare_fusion
  44.7 77.9 %reduce-scatter.5.cloned.1.call-done = f32[64,1792]{1,0:T(8,128)} async-done(((f32[1024,1792]{1,0:T(8,128)}), f32[64,1792]{1,0:T(8,128)}) %reduce-scatter.5.cloned.1.call-update) | async-done | bytes 458768 | tf_op jit(solution)/shard_map/reduce_scatter | solution.py:255
  122.6 91.9 %reduce-scatter.3.cloned.1.call-done = f32[64,1792]{1,0:T(8,128)} async-done(((f32[1024,1792]{1,0:T(8,128)}), f32[64,1792]{1,0:T(8,128)}) %reduce-scatter.3.cloned.1.call-update) | async-done | bytes 458768 | tf_op jit(solution)/shard_map/reduce_scatter | solution.py:253
  214.5 1.3 multiply_convert_fusion
  215.8 0.1 slice_bitcast_fusion
  215.9 0.7 pad_maximum_fusion.own_ref
  216.6 23.6 %gather_col.1 = bf16[16,2,32,1792]{3,2,1,0:T(8,128)(2,1)} custom-call(bf16[2,32,1792]{2,1,0:T(8,128)(2,1)} %pad_maximum_fusion.own_ref), custom_call_target="tpu_custom_call" | custom-call | tf_op jit(solution)/shard_map/gather_col/pallas_call | solution.py:176
  240.3 6.0 %fusion.part_ref = f32[16,2,32,512]{3,2,1,0:T(8,128)} fusion(bf16[16,2,32,1792]{3,2,1,0:T(8,128)(2,1)} %gather_col.1, bf16[1792,512]{1,0:T(8,128)(2,1)} %param.11), kind=kOutput, calls=%fused_computation | convolution fusion | flops 1879048192 | bytes 7602176 | tf_op jit(solution)/shard_map/dot_general | solution.py:260
  246.3 25.7 %scatter_row.1 = (f32[32,512]{1,0:T(8,128)}, f32[32,512]{1,0:T(8,128)}) custom-call(f32[16,2,32,512]{3,2,1,0:T(8,128)} %fusion.part_ref), custom_call_target="tpu_custom_call" | custom-call | tf_op jit(solution)/shard_map/scatter_row/pallas_call | solution.py:230
  272.0 1.5 copy.11
  273.4 1.5 copy.12
Async XLA Ops:
  7.2 22.7 %copy-start = (bf16[512,1792]{1,0:T(8,128)(2,1)S(1)}, bf16[512,1792]{1,0:T(8,128)(2,1)}, u32[]{:S(2)}) copy-start(bf16[512,1792]{1,0:T(8,128)(2,1)} %param.10) | copy-start | bytes 5505028
  7.2 115.4 %reduce-scatter.5.cloned.1.call-start = ((), (), s32[]{:S(2)}) async-start(), calls=%async_computation.3 | async-start | bytes 7798784 | tf_op jit(solution)/shard_map/reduce_scatter | solution.py:255
  36.1 1.2 copy-start.1
  36.1 178.4 %reduce-scatter.3.cloned.1.call-start = ((), (), s32[]{:S(2)}) async-start(), calls=%async_computation.2 | async-start | bytes 7798784 | tf_op jit(solution)/shard_map/reduce_scatter | solution.py:253
Sparse Core Ops, SparseCore 0:
  36.2 86.3 reduce-scatter.4
  126.4 88.1 reduce-scatter.2

commit v2 on v1

--- a/solution.py
+++ b/solution.py
@@ -246,13 +246,132 @@
     )(part)
 
 
+def scatter_col_kernel(gate_ref, up_ref, gate_out, up_out, far, free, dep, mid, far2, free2, dep2, send1, recv1, send2, recv2):
+    me = lax.axis_index("col")
+    y, x = me // XN, me % XN
+    parts, outs = (gate_ref, up_ref), (gate_out, up_out)
+    half = gate_ref.shape[1] // 2
+    rows = (pl.ds(0, half), pl.ds(half, half))
+    lanes = (1, XN - 1)
+
+    def at(dy, dx):
+        return ((y + dy) % XN) * XN + (x + dx) % XN
+
+    def block(run, lane, hop):
+        return at(hop, lane) if run == 0 else at(lane, hop)
+
+    started = []
+
+    def go(copy):
+        copy.start()
+        started.append(copy)
+
+    def first(kind, run, way, j):
+        if kind == 0:
+            src, dst = parts[run].at[block(run, 2, j), rows[way]], far.at[run, way, j]
+        elif kind == 1:
+            src, dst = far.at[run, way, j], dep.at[run, way, j]
+        else:
+            src, dst = parts[run].at[block(run, lanes[way], j), rows[1 - way]], free.at[run, way, j]
+        sems = (kind, run, way, j)
+        return remote(src, dst, send1.at[sems], recv1.at[sems], "col", block(run, lanes[way], 0))
+
+    def second(kind, run, way):
+        if kind == 0:
+            src, dst = mid.at[run, 2, rows[way]], far2.at[run, way]
+        elif kind == 1:
+            src, dst = far2.at[run, way], dep2.at[run, way]
+        else:
+            src, dst = mid.at[run, lanes[way], rows[1 - way]], free2.at[run, way]
+        sems = (kind, run, way)
+        return remote(src, dst, send2.at[sems], recv2.at[sems], "col", block(run, 0, lanes[way]))
+
+    both = [(run, way) for way in range(2) for run in range(2)]
+
+    def passes(j):
+        for run, way in both:
+            first(0, run, way, j).wait_recv()
+            far[run, way, j] += parts[run][block(run, lanes[way], j), rows[way]]
+            go(first(1, run, way, j))
+        for run, way in both:
+            go(first(2, run, way, j))
+
+    def totals(j):
+        for run, way in both:
+            first(1, run, way, j).wait_recv()
+            first(2, run, way, j).wait_recv()
+        for run in range(2):
+            mine = block(run, 0, j)
+            for way in range(2):
+                mid[run, j, rows[way]] = parts[run][mine, rows[way]] + dep[run, way, j] + free[run, 1 - way, j]
+
+    greet("col", (at(0, 1), at(0, XN - 1), at(1, 0), at(XN - 1, 0)))
+    for j in (2, 1):
+        for run, way in both:
+            go(first(0, run, way, j))
+    passes(2)
+    for run, way in both:
+        go(first(0, run, way, 3))
+    passes(1)
+    for run, way in both:
+        go(first(0, run, way, 0))
+    passes(3)
+    totals(2)
+    for run, way in both:
+        go(second(0, run, way))
+    passes(0)
+    totals(1)
+    for run in range(2):
+        go(second(2, run, 0))
+    totals(3)
+    for run in range(2):
+        go(second(2, run, 1))
+    for run, way in both:
+        second(0, run, way).wait_recv()
+        far2[run, way] += mid[run, lanes[way], rows[way]]
+        go(second(1, run, way))
+    totals(0)
+    for run, way in both:
+        second(1, run, way).wait_recv()
+        second(2, run, way).wait_recv()
+    for run, way in both:
+        outs[run][rows[way]] = mid[run, 0, rows[way]] + dep2[run, way] + free2[run, 1 - way]
+    for copy in started:
+        copy.wait_send()
+
+
+def scatter_col(gate_part, up_part):
+    count, rows, width = gate_part.shape
+    out = jax.ShapeDtypeStruct((rows, width), jnp.float32)
+    wide = pltpu.VMEM((2, 2, XN, rows // 2, width), jnp.float32)
+    slim = pltpu.VMEM((2, 2, rows // 2, width), jnp.float32)
+    vmem = pl.BlockSpec(memory_space=pltpu.VMEM)
+    return pl.pallas_call(
+        scatter_col_kernel,
+        out_shape=(out, out),
+        in_specs=[vmem, vmem],
+        out_specs=(vmem, vmem),
+        scratch_shapes=[
+            wide, wide, wide,
+            pltpu.VMEM((2, XN, rows, width), jnp.float32),
+            slim, slim, slim,
+            pltpu.SemaphoreType.DMA((3, 2, 2, XN)),
+            pltpu.SemaphoreType.DMA((3, 2, 2, XN)),
+            pltpu.SemaphoreType.DMA((3, 2, 2)),
+            pltpu.SemaphoreType.DMA((3, 2, 2)),
+        ],
+        compiler_params=pltpu.CompilerParams(collective_id=3, has_side_effects=True, vmem_limit_bytes=48 << 20),
+        name="scatter_col",
+    )(gate_part, up_part)
+
+
 def on_device(clean_in, corrupt_in, patch_mask, gate_weight, up_weight, down_weight):
     rows, width = clean_in.shape
     piece = gather_row(clean_in, corrupt_in).reshape(-1, width)
     gate_part = jnp.dot(piece, gate_weight, preferred_element_type=jnp.float32)
-    gate = lax.psum_scatter(gate_part, "col", scatter_dimension=0, tiled=True)
     up_part = jnp.dot(piece, up_weight, preferred_element_type=jnp.float32)
-    up = lax.psum_scatter(up_part, "col", scatter_dimension=0, tiled=True)
+    split = (XN * XN, 2 * rows, -1)
+    gate, up = scatter_col(gate_part.reshape(split), up_part.reshape(split))
     row_mask = lax.dynamic_slice_in_dim(patch_mask, lax.axis_index("col") * rows, rows, 0)
     hidden = (jax.nn.silu(gate) * up).astype(jnp.bfloat16).reshape(2, rows, -1)
     patched = jnp.where(row_mask[:, None] == 1, hidden[0], hidden[1])

time: 282 us -> 179 us (0.63)
  waiting for transfers between devices: 170 us -> 0 us
  Pallas kernels: 71.9 us -> 156 us
  between operations: 14.1 us -> 0.71 us
    reduce_scatter x2 -> x0, waiting for transfers between devices: 170 us -> none  [the longest x1 91.9 us: on_device(): gate = lax.psum_scatter(gate_part, 'col', scatter_dimension=0, tiled=True)]
    pallas_call x0 -> x1, Pallas kernels: none -> 86.1 us  [scatter_col(): pl.pallas_call(scatter_col_kernel, out_shape=(out, out), in_specs=[vmem,...]
  transfers between devices with their start and end apart: 2 -> 0, of which waited for: 2 -> 0; matrix products, arithmetic and copies ran while one was open for 3% -> 0% of each run, Pallas kernels for 0% -> 0%
where the time goes in v2:
time: 179 us; the launch traced here: 178 us
  Pallas kernels  156 us (87%)
  matrix products  17.5 us (10%)
  local copies, waits for them, and re-layouts  2.97 us (2%)
    pallas_call x1, Pallas kernels, scatter_col(): pl.pallas_call(scatter_col_kernel, out_shape=(out, out), in_specs=[vmem,...  86.1 us
    pallas_call x1, Pallas kernels, scatter_row(): pl.pallas_call(scatter_row_kernel, out_shape=(out, out), in_specs=[pl.Blo...  23.6 us
    pallas_call x1, Pallas kernels, gather_col(): pl.pallas_call(gather_col_kernel, out_shape=jax.ShapeDtypeStruct((XN * XN...  23.3 us
    pallas_call x1, Pallas kernels, gather_row(): pl.pallas_call(gather_row_kernel, out_shape=jax.ShapeDtypeStruct((2 * ZN,...  22.6 us
    dot_general x1, matrix products, on_device(): up_part = jnp.dot(piece, up_weight, preferred_element_type=jnp.float32)  6.38 us
    dot_general x1, matrix products, on_device(): jnp.dot(gathered.reshape(-1, gathered.shape[-1]), down_weight, preferred_...  6.01 us
    dot_general x1, matrix products, on_device(): gate_part = jnp.dot(piece, gate_weight, preferred_element_type=jnp.float32)  5.08 us

profile of v2, /device:TPU:1, one launch (start us, length us, event | category | flops | bytes accessed | tf_op | source)
XLA Modules:
  0.0 178.5 jit_solution(10723724195601225143)
XLA Ops:
  0.6 0.0 copy-start
  0.6 22.6 %gather_row.1 = bf16[16,2,32,512]{3,2,1,0:T(8,128)(2,1)} custom-call(bf16[32,512]{1,0:T(8,128)(2,1)} %clean_ref.1, bf16[32,512]{1,0:T(8,128)(2,1)} %corrupt_ref.1), custom_call_target="tpu_custom_call" | custom-call | tf_op jit(solution)/shard_map/gather_row/pallas_call | solution.py:79
  23.3 0.0 copy-done
  23.3 0.0 copy-start.1
  23.3 0.0 copy-start.2
  23.3 6.4 %fusion.2.up_ref = f32[16,64,1792]{2,1,0:T(8,128)} fusion(bf16[16,64,512]{2,1,0:T(8,128)(2,1)} %bitcast.19, bf16[512,1792]{1,0:T(8,128)(2,1)S(1)} %copy-done), kind=kOutput, calls=%fused_computation.2 | convolution fusion | flops 1879048192 | bytes 10223616 | tf_op jit(solution)/shard_map/dot_general | solution.py:372
  29.7 0.0 copy-done.1
  29.7 0.0 copy-done.2
  29.7 5.1 %fusion.4.gate_ref = f32[16,64,1792]{2,1,0:T(8,128)} fusion(bf16[16,64,512]{2,1,0:T(8,128)(2,1)S(1)} %bitcast.20, bf16[512,1792]{1,0:T(8,128)(2,1)S(1)} %copy-done.2), kind=kOutput, calls=%fused_computation.4 | convolution fusion | flops 1879048192 | bytes 10223616 | tf_op jit(solution)/shard_map/dot_general | solution.py:371
  34.8 86.1 %scatter_col.1 = (f32[64,1792]{1,0:T(8,128)S(1)}, f32[64,1792]{1,0:T(8,128)S(1)}) custom-call(f32[16,64,1792]{2,1,0:T(8,128)} %fusion.4.gate_ref, f32[16,64,1792]{2,1,0:T(8,128)} %fusion.2.up_ref), custom_call_target="tpu_custom_call" | custom-call | tf_op jit(solution)/shard_map/scatter_col/pallas_call | solution.py:349
  120.9 0.1 multiply_convert_fusion
  121.0 0.8 dynamic-slice_compare_fusion
  121.8 0.1 slice_bitcast_fusion
  121.9 0.7 pad_maximum_fusion.own_ref
  122.6 23.3 %gather_col.1 = bf16[16,2,32,1792]{3,2,1,0:T(8,128)(2,1)} custom-call(bf16[2,32,1792]{2,1,0:T(8,128)(2,1)} %pad_maximum_fusion.own_ref), custom_call_target="tpu_custom_call" | custom-call | tf_op jit(solution)/shard_map/gather_col/pallas_call | solution.py:176
  145.9 6.0 %fusion.part_ref = f32[16,2,32,512]{3,2,1,0:T(8,128)} fusion(bf16[16,2,32,1792]{3,2,1,0:T(8,128)(2,1)} %gather_col.1, bf16[1792,512]{1,0:T(8,128)(2,1)} %param.11), kind=kOutput, calls=%fused_computation | convolution fusion | flops 1879048192 | bytes 7602176 | tf_op jit(solution)/shard_map/dot_general | solution.py:379
  151.9 23.6 %scatter_row.1 = (f32[32,512]{1,0:T(8,128)}, f32[32,512]{1,0:T(8,128)}) custom-call(f32[16,2,32,512]{3,2,1,0:T(8,128)} %fusion.part_ref), custom_call_target="tpu_custom_call" | custom-call | tf_op jit(solution)/shard_map/scatter_row/pallas_call | solution.py:230
  175.5 1.5 copy.11
  177.0 1.5 copy.12
Async XLA Ops:
  0.6 22.7 %copy-start = (bf16[512,1792]{1,0:T(8,128)(2,1)S(1)}, bf16[512,1792]{1,0:T(8,128)(2,1)}, u32[]{:S(2)}) copy-start(bf16[512,1792]{1,0:T(8,128)(2,1)} %param.10) | copy-start | bytes 5505028
  23.3 6.4 %copy-start.1 = (bf16[16,2,32,512]{3,2,1,0:T(8,128)(2,1)S(1)}, bf16[16,2,32,512]{3,2,1,0:T(8,128)(2,1)}, u32[]{:S(2)}) copy-start(bf16[16,2,32,512]{3,2,1,0:T(8,128)(2,1)} %gather_row.1) | copy-start | bytes 3145732
  23.3 6.4 %copy-start.2 = (bf16[512,1792]{1,0:T(8,128)(2,1)S(1)}, bf16[512,1792]{1,0:T(8,128)(2,1)}, u32[]{:S(2)}) copy-start(bf16[512,1792]{1,0:T(8,128)(2,1)} %param.9) | copy-start | bytes 5505028
